TPU v7x, 256 devices: a whole 4x4x8 slice. The times are simulated.
256 devices in a mesh: expert: 64 (over y, z, core), half: 4 (over x).
Axes of the slice: x: 4, y: 4, z: 8, core: 2. Of those that a mesh axis runs over, the one named last changes fastest.
Arguments:
- tokens: bfloat16 [8192, 2048], P('expert', 'half'), may hold values from -6 to 6
- cotangent: bfloat16 [8192, 2048], P('expert', 'half'), may hold values from -4 to 4
- route: int32 [8192, 8], P('expert'), may hold values from 0 to 127, all different within a row; in each aligned block of 128 rows (0 to 127, 128 to 255, ...) at most 16 rows name the same one
- prob: bfloat16 [8192, 8], P('expert'), may hold values from 0.19921875 to 1
- w_gate: bfloat16 [128, 768, 2048], P('expert', 'half'), may hold values from -0.125 to 0.125
- w_up: bfloat16 [128, 768, 2048], P('expert', 'half'), may hold values from -0.125 to 0.125
- w_down: bfloat16 [128, 768, 2048], P('expert', 'half'), may hold values from -0.21875 to 0.21875
Outputs:
- grad_tokens: bfloat16 [8192, 2048], P('expert', 'half')
- grad_prob: float32 [8192, 8], P('expert')
- grad_gate: bfloat16 [128, 768, 2048], P('expert', 'half')
- grad_up: bfloat16 [128, 768, 2048], P('expert', 'half')
- grad_down: bfloat16 [128, 768, 2048], P('expert', 'half')
Inputs may be any that keep to these rules, and one draw needn't show every extreme that they name: `route`: each row names 8 different experts; among the rows of one device no expert is named more than 16 times, and that most is reached.
All inputs are finite; a program needn't handle non-finite values.
Results may differ from a plain program's by a relative error of at most 0.013.
Values may be sent and summed in bfloat16 or wider, within the bound.
No kernel may reach another device: no remote copies, remote signals or barrier semaphores. Data moves between devices by JAX's collectives and lax.ppermute only.
A program may use at most 192 MiB of HBM per device.

v0:
```python
import jax
import jax.numpy as jnp
from jax import lax
from jax.sharding import PartitionSpec as P


def per_device(tokens, cotangent, route, prob, w_gate, w_up, w_down):
    tok_rows = route.shape[0]
    top = route.shape[1]
    local_exp = w_gate.shape[0]
    groups = lax.axis_size("expert")
    experts = local_exp * groups
    capacity = 2 * tok_rows * top // experts
    slots = experts * capacity
    flat_route = route.reshape(-1)
    hits = (flat_route[:, None] == jnp.arange(experts, dtype=jnp.int32)[None, :]).astype(jnp.int32)
    rank = jnp.sum((jnp.cumsum(hits, axis=0) - hits) * hits, axis=1)
    slot_of = flat_route * capacity + rank
    source = (
        jnp.zeros((slots,), jnp.int32).at[slot_of].set(jnp.arange(tok_rows * top, dtype=jnp.int32))
    )
    filled = jnp.zeros((slots,), jnp.bool_).at[slot_of].set(True)
    token_of = source // top
    slot_prob = jnp.where(filled, prob.reshape(-1)[source], jnp.zeros((), jnp.bfloat16))
    slot_prob = slot_prob.reshape(groups, local_exp * capacity)

    def pack(rows):
        picked = jnp.where(filled[:, None], rows[token_of], jnp.zeros((), jnp.bfloat16))
        return picked.reshape(groups, local_exp * capacity, rows.shape[1])

    sent_x, sent_d, recv_p = (
        lax.all_to_all(pack(tokens), "expert", split_axis=0, concat_axis=0, tiled=True),
        lax.all_to_all(pack(cotangent), "expert", split_axis=0, concat_axis=0, tiled=True),
        lax.all_to_all(slot_prob, "expert", split_axis=0, concat_axis=0, tiled=True),
    )
    recv_x, recv_d = (
        lax.all_gather(sent_x, "half", axis=2, tiled=True),
        lax.all_gather(sent_d, "half", axis=2, tiled=True),
    )
    width = recv_x.shape[2]
    xin = recv_x.reshape(groups, local_exp, capacity, width)
    dout = recv_d.reshape(groups, local_exp, capacity, width)
    weight = recv_p.reshape(groups, local_exp, capacity).astype(jnp.float32)
    gate = jnp.einsum("gecd,efd->gecf", xin, w_gate, preferred_element_type=jnp.float32)
    upval = jnp.einsum("gecd,efd->gecf", xin, w_up, preferred_element_type=jnp.float32)
    sig = jax.nn.sigmoid(gate)
    act = gate * sig
    hidden = (act * upval).astype(jnp.bfloat16)
    raw = jnp.einsum("gecd,efd->gecf", dout, w_down, preferred_element_type=jnp.float32)
    score = jnp.sum(hidden.astype(jnp.float32) * raw, axis=3)
    scaled = (weight[..., None] * dout.astype(jnp.float32)).astype(jnp.bfloat16)
    dact = weight[..., None] * raw
    dgate = (dact * upval * sig * (1.0 + gate * (1.0 - sig))).astype(jnp.bfloat16)
    dup = (dact * act).astype(jnp.bfloat16)
    grad_down = jnp.einsum(
        "gecf,gecd->efd", hidden, scaled, preferred_element_type=jnp.float32
    ).astype(jnp.bfloat16)
    grad_gate = jnp.einsum("gecf,gecd->efd", dgate, xin, preferred_element_type=jnp.float32).astype(
        jnp.bfloat16
    )
    grad_up = jnp.einsum("gecf,gecd->efd", dup, xin, preferred_element_type=jnp.float32).astype(
        jnp.bfloat16
    )
    part = jnp.einsum("gecf,efd->gecd", dgate, w_gate, preferred_element_type=jnp.float32)
    part = (
        part + jnp.einsum("gecf,efd->gecd", dup, w_up, preferred_element_type=jnp.float32)
    ).astype(jnp.bfloat16)
    summed = lax.psum_scatter(
        part.astype(jnp.float32).astype(jnp.bfloat16), "half", scatter_dimension=3, tiled=True
    ).astype(jnp.float32)
    total_score = lax.psum(score, "half")
    quarter = summed.shape[3]
    back_rows, back_score = (
        lax.all_to_all(
            summed.reshape(groups, local_exp * capacity, quarter).astype(jnp.bfloat16),
            "expert",
            split_axis=0,
            concat_axis=0,
            tiled=True,
        ).astype(jnp.float32),
        lax.all_to_all(
            total_score.reshape(groups, local_exp * capacity).astype(jnp.bfloat16),
            "expert",
            split_axis=0,
            concat_axis=0,
            tiled=True,
        ).astype(jnp.float32),
    )
    picked = back_rows.reshape(slots, quarter)[slot_of].reshape(tok_rows, top, quarter)
    grad_tokens = jnp.sum(picked, axis=1).astype(jnp.bfloat16)
    grad_prob = back_score.reshape(slots)[slot_of].reshape(tok_rows, top)
    return (grad_tokens, grad_prob, grad_gate, grad_up, grad_down)


def solution(mesh):
    in_specs = (
        P("expert", "half"),
        P("expert", "half"),
        P("expert", None),
        P("expert", None),
        P("expert", "half", None),
        P("expert", "half", None),
        P("expert", "half", None),
    )
    out_specs = (
        P("expert", "half"),
        P("expert", None),
        P("expert", "half", None),
        P("expert", "half", None),
        P("expert", "half", None),
    )
    return jax.shard_map(
        per_device, mesh=mesh, in_specs=in_specs, out_specs=out_specs, check_vma=False
    )
```

profile of v0, /device:TPU:1, one launch (start us, length us, event | category | flops | bytes accessed | tf_op | source)
XLA Modules:
  0.0 475.6 jit_solution(6018880050518364092)
XLA Ops:
  7.2 0.0 copy-start
  7.2 0.0 all-gather.5.cloned.1.call-start
  7.2 0.8 broadcast_multiply_fusion
  8.1 0.8 copy.60
  8.8 0.1 eq.29
  8.9 0.1 eq.25
  9.0 0.1 copy.59
  9.1 0.1 mul.61
  9.2 0.1 copy.62
  9.3 0.2 fusion.36
  9.6 0.1 copy.63
  9.7 0.4 fusion.35
  10.1 4.3 scatter_custom_fusion.1
  14.5 4.3 scatter_custom_fusion
  18.8 0.1 broadcast_in_dim.48
  18.9 0.0 copy-start.3
  18.9 9.2 %gather_fusion.2 = bf16[2048,512]{1,0:T(8,128)(2,1)} fusion(bf16[128,512]{1,0:T(8,128)(2,1)S(1)} %copy-done.2, s32[2048]{0:T(1024)S(1)} %get-tuple-element.25), kind=kCustom, calls=%fused_computation.2 | custom fusion | bytes 4202496 | tf_op jit(solution)/shard_map/gather | solution.py:28
  28.1 9.2 %gather_fusion.1 = bf16[2048,512]{1,0:T(8,128)(2,1)} fusion(bf16[128,512]{1,0:T(8,128)(2,1)S(1)} %copy-done.3, s32[2048]{0:T(1024)S(1)} %get-tuple-element.25), kind=kCustom, calls=%fused_computation.1 | custom fusion | bytes 4202496 | tf_op jit(solution)/shard_map/gather | solution.py:28
  37.3 3.4 broadcast_select_fusion.1
  40.8 64.3 %all_to_all.31 = bf16[64,32,512]{2,1,0:T(8,128)(2,1)} all-to-all(bf16[64,32,512]{2,1,0:T(8,128)(2,1)S(1)} %get-tuple-element.27), channel_id=1, replica_groups=mesh['expert'=64,'half'=4] {'expert'}, dimensions={0} | all-to-all | bytes 4194304 | tf_op jit(solution)/shard_map/all_to_all | solution.py:32
  105.1 0.0 all-gather.5.cloned.1.call-update
  105.1 0.0 all-gather.3.cloned.1.call-start
  105.1 57.2 %all_to_all.32 = bf16[64,32,512]{2,1,0:T(8,128)(2,1)} all-to-all(bf16[64,32,512]{2,1,0:T(8,128)(2,1)} %get-tuple-element.26), channel_id=1, replica_groups=mesh['expert'=64,'half'=4] {'expert'}, dimensions={0} | all-to-all | bytes 4194304 | tf_op jit(solution)/shard_map/all_to_all | solution.py:33
  162.3 0.0 all-gather.3.cloned.1.call-update
  162.3 0.0 reduce-scatter.2.cloned.1.call-start
  162.4 0.6 copy-done.9
  163.0 0.1 copy.64
  163.1 0.1 reshape.125
  163.2 13.1 %gather_fusion = bf16[2048]{0:T(1024)(128)(2,1)S(1)} fusion(bf16[1024]{0:T(1024)(128)(2,1)S(1)} %reshape.125, s32[2048]{0:T(1024)S(1)} %get-tuple-element.24), kind=kCustom, calls=%fused_computation | custom fusion | bytes 16384 | tf_op jit(solution)/shard_map/gather | solution.py:24
  176.3 0.1 all_to_all.25
  176.4 14.9 %all_to_all.33 = bf16[64,1,32]{2,1,0:T(2,128)(2,1)S(1)} all-to-all(bf16[64,1,32]{2,1,0:T(2,128)(2,1)S(1)} %all_to_all.25), channel_id=1, replica_groups=mesh['expert'=64,'half'=4] {'expert'}, dimensions={0} | all-to-all | bytes 8192 | tf_op jit(solution)/shard_map/all_to_all | solution.py:34
  191.3 0.1 copy.66
  191.4 0.1 copy.67
  191.5 0.0 all-gather.5.cloned.1.call-done
  191.5 0.0 copy-start.4
  191.6 7.2 %fusion.9 = f32[2,64,16,192]{3,2,1,0:T(8,128)} fusion(bf16[64,2,16,2048]{3,2,1,0:T(8,128)(2,1)} %bitcast.121, bf16[2,192,2048]{2,1,0:T(8,128)(2,1)S(1)} %copy-done), kind=kOutput, calls=%fused_computation.18 | convolution fusion | flops 1610612736 | bytes 11534336 | tf_op jit(solution)/shard_map/gecd,efd->gecf/dot_general | solution.py:44
  198.8 3.7 fusion.11
  202.5 73.4 %all-gather.3.cloned.1.call-done = bf16[64,32,2048]{2,1,0:T(8,128)(2,1)} async-done(((bf16[64,32,512]{2,1,0:T(8,128)(2,1)}), bf16[64,32,2048]{2,1,0:T(8,128)(2,1)}) %all-gather.3.cloned.1.call-update) | async-done | bytes 8388624 | tf_op jit(solution)/shard_map/all_gather | solution.py:38
  275.8 9.4 %fusion.27 = (f32[64,2,16]{2,0,1:T(8,128)S(1)}, bf16[64,2,16,192]{3,2,0,1:T(8,128)(2,1)}, bf16[64,2,16,192]{3,2,0,1:T(8,128)(2,1)S(1)}, bf16[64,2,16,192]{3,2,0,1:T(8,128)(2,1)S(1)}) fusion(f32[2,64,16,192]{3,2,1,0:T(8,128)} %fusion.11, f32[2,64,16,192]{3,2,1,0:T(8,128)} %fusion.9, f32[64,2,16]{2,0,1:T(8,128)S(1)} %copy.67, ...), kind=kOutput, calls=%fused_computation.42 | convolution fusion | flops 1618081792 | bytes 15482880 | tf_op jit(solution)/shard_map/gecd,efd->gecf/dot_general | solution.py:49
  285.2 8.1 %fusion.28 = f32[2,64,16,2048]{3,2,1,0:T(8,128)} fusion(bf16[64,2,16,192]{3,2,0,1:T(8,128)(2,1)S(1)} %get-tuple-element.22, bf16[2,192,2048]{2,1,0:T(8,128)(2,1)S(1)} %copy-done), kind=kOutput, calls=%fused_computation.46 | convolution fusion | flops 1610612736 | bytes 19136512 | tf_op jit(solution)/shard_map/gecf,efd->gecd/dot_general | solution.py:64
  293.3 11.6 %fusion = bf16[64,2,16,2048]{3,2,0,1:T(8,128)(2,1)} fusion(f32[2,64,16,2048]{3,2,1,0:T(8,128)} %fusion.28, bf16[64,2,16,192]{3,2,0,1:T(8,128)(2,1)S(1)} %get-tuple-element.23, bf16[2,192,2048]{2,1,0:T(8,128)(2,1)S(1)} %copy-done.4), kind=kOutput, calls=%fused_computation.9 | convolution fusion | flops 1619001344 | bytes 27525120 | tf_op jit(solution)/shard_map/gecf,efd->gecd/dot_general | solution.py:66
  304.8 0.0 reduce-scatter.2.cloned.1.call-update
  304.9 0.1 copy.76
  305.0 0.1 copy.72
  305.1 12.0 %psum.7 = bf16[64,2,16]{0,2,1:T(8,128)(2,1)S(1)} all-reduce(f32[64,2,16]{0,2,1:T(8,128)S(1)} %copy.72), channel_id=1, replica_groups=mesh['expert'=64,'half'=4] {'half'}, use_global_device_ids=true, to_apply=%region_8.9 | all-reduce | flops 2048 | bytes 12288 | tf_op jit(solution)/shard_map/psum | solution.py:71
  317.1 0.7 copy.73
  317.8 14.8 %all-to-all-start.4 = ((bf16[64,1,32]{2,1,0:T(2,128)(2,1)}), bf16[64,1,32]{2,1,0:T(2,128)(2,1)S(1)}, u32[]{:S(2)}, u32[]{:S(2)}) async-start(bf16[64,1,32]{2,1,0:T(2,128)(2,1)} %copy.73), calls=%async_computation.5 | async-start | bytes 65536 | tf_op jit(solution)/shard_map/all_to_all | solution.py:81
  332.6 6.4 %bitcast_convert_fusion.2 = bf16[2,192,2048]{2,1,0:T(8,128)(2,1)} fusion(bf16[64,2,16,192]{3,2,0,1:T(8,128)(2,1)S(1)} %copy-done.6, bf16[64,2,16,2048]{3,2,1,0:T(8,128)(2,1)} %bitcast.122), kind=kOutput, calls=%fused_computation.24 | convolution fusion | flops 1611399168 | bytes 10747904 | tf_op jit(solution)/shard_map/gecf,gecd->efd/dot_general | solution.py:58
  339.0 50.2 %reduce-scatter.2.cloned.1.call-done = bf16[64,2,16,512]{3,2,0,1:T(8,128)(2,1)} async-done(((bf16[64,2,16,2048]{3,2,0,1:T(8,128)(2,1)}), bf16[64,2,16,512]{3,2,0,1:T(8,128)(2,1)}) %reduce-scatter.2.cloned.1.call-update) | async-done | bytes 2097168 | tf_op jit(solution)/shard_map/reduce_scatter | solution.py:68
  389.2 3.2 copy.71
  392.4 0.0 all-to-all-done.4
  392.4 11.0 %all-to-all-start.3 = ((bf16[64,32,512]{2,1,0:T(8,128)(2,1)}), bf16[64,32,512]{2,1,0:T(8,128)(2,1)}, u32[]{:S(2)}, u32[]{:S(2)}) async-start(bf16[64,32,512]{2,1,0:T(8,128)(2,1)} %bitcast.113), calls=%async_computation.4 | async-start | bytes 4194304 | tf_op jit(solution)/shard_map/all_to_all | solution.py:74
  403.4 0.0 copy-start.11
  403.4 6.4 %bitcast_convert_fusion.1 = bf16[2,192,2048]{2,1,0:T(8,128)(2,1)} fusion(bf16[64,2,16,192]{3,2,0,1:T(8,128)(2,1)S(1)} %copy-done.8, bf16[64,2,16,2048]{3,2,1,0:T(8,128)(2,1)} %bitcast.123), kind=kOutput, calls=%fused_computation.23 | convolution fusion | flops 1611399168 | bytes 10747904 | tf_op jit(solution)/shard_map/gecf,gecd->efd/dot_general | solution.py:61
  409.8 5.5 %bitcast_convert_fusion = bf16[2,192,2048]{2,1,0:T(8,128)(2,1)} fusion(bf16[64,2,16,192]{3,2,0,1:T(8,128)(2,1)S(1)} %copy-done.11, f32[64,2,16]{2,1,0:T(2,128)S(1)} %copy.76, bf16[64,32,2048]{2,1,0:T(8,128)(2,1)} %all-gather.3.cloned.1.call-done), kind=kOutput, calls=%fused_computation.22 | convolution fusion | flops 1623982080 | bytes 10756096 | tf_op jit(solution)/shard_map/gecf,gecd->efd/dot_general | solution.py:55
  415.3 0.1 convert_reduce_fusion
  415.4 0.1 reshape.135
  415.5 6.1 %gather_fusion.4 = f32[1024]{0:T(1024)S(1)} fusion(f32[2048]{0:T(1024)S(1)} %reshape.135, s32[1024]{0:T(1024)S(1)} %broadcast_clamp_fusion), kind=kCustom, calls=%fused_computation.4 | custom fusion | bytes 12288 | tf_op jit(solution)/shard_map/gather | solution.py:91
  421.7 0.1 reshape.131
  421.7 0.7 copy.78
  422.4 32.1 %all-to-all-done.3 = bf16[64,32,512]{2,1,0:T(8,128)(2,1)} async-done(((bf16[64,32,512]{2,1,0:T(8,128)(2,1)}), bf16[64,32,512]{2,1,0:T(8,128)(2,1)}, u32[]{:S(2)}, u32[]{:S(2)}) %all-to-all-start.3) | async-done | bytes 2097184 | tf_op jit(solution)/shard_map/all_to_all | solution.py:74
  454.5 4.1 bitcast_convert_fusion.3
  458.6 7.6 %gather_fusion.3 = f32[1024,512]{1,0:T(8,128)} fusion(f32[2048,512]{1,0:T(8,128)} %bitcast_convert_fusion.3, s32[1024]{0:T(1024)S(1)} %broadcast_clamp_fusion), kind=kCustom, calls=%fused_computation.3 | custom fusion | bytes 4198400 | tf_op jit(solution)/shard_map/gather | solution.py:89
  466.3 2.8 bitcast_reduce_fusion
  (29 shorter events, 0.2 us)
Async XLA Ops:
  7.2 184.4 %copy-start = (bf16[2,192,2048]{2,1,0:T(8,128)(2,1)S(1)}, bf16[2,192,2048]{2,1,0:T(8,128)(2,1)}, u32[]{:S(2)}) copy-start(bf16[2,192,2048]{2,1,0:T(8,128)(2,1)} %param.11) | copy-start | bytes 4718596
  7.2 11.7 %copy-start.2 = (bf16[128,512]{1,0:T(8,128)(2,1)S(1)}, bf16[128,512]{1,0:T(8,128)(2,1)}, u32[]{:S(2)}) copy-start(bf16[128,512]{1,0:T(8,128)(2,1)} %param.7) | copy-start | bytes 393220
  7.2 184.3 %all-gather.5.cloned.1.call-start = ((), (), s32[]{:S(2)}) async-start(), calls=%async_computation.7 | async-start | bytes 10485760 | tf_op jit(solution)/shard_map/all_gather | solution.py:37
  18.9 9.2 %copy-start.3 = (bf16[128,512]{1,0:T(8,128)(2,1)S(1)}, bf16[128,512]{1,0:T(8,128)(2,1)}, u32[]{:S(2)}) copy-start(bf16[128,512]{1,0:T(8,128)(2,1)} %param.8) | copy-start | bytes 393220
  105.1 170.7 %all-gather.3.cloned.1.call-start = ((), (), s32[]{:S(2)}) async-start(), calls=%async_computation.6 | async-start | bytes 10485760 | tf_op jit(solution)/shard_map/all_gather | solution.py:38
  162.3 0.7 copy-start.9
  162.3 226.8 %reduce-scatter.2.cloned.1.call-start = ((), (), s32[]{:S(2)}) async-start(), calls=%async_computation.8 | async-start | bytes 10485760 | tf_op jit(solution)/shard_map/reduce_scatter | solution.py:68
  191.5 7.2 %copy-start.4 = (bf16[2,192,2048]{2,1,0:T(8,128)(2,1)S(1)}, bf16[2,192,2048]{2,1,0:T(8,128)(2,1)}, u32[]{:S(2)}) copy-start(bf16[2,192,2048]{2,1,0:T(8,128)(2,1)} %param.12) | copy-start | bytes 4718596
  191.6 7.2 %copy-start.10 = (bf16[64,32,2048]{2,1,0:T(8,128)(2,1)S(1)}, bf16[64,32,2048]{2,1,0:T(8,128)(2,1)}, u32[]{:S(2)}) copy-start(bf16[64,32,2048]{2,1,0:T(8,128)(2,1)} %all-gather.5.cloned.1.call-done) | copy-start | bytes 25165828
  285.2 8.1 %copy-start.5 = (bf16[64,2,16,192]{3,2,0,1:T(8,128)(2,1)}, bf16[64,2,16,192]{3,2,0,1:T(8,128)(2,1)S(1)}, u32[]{:S(2)}) copy-start(bf16[64,2,16,192]{3,2,0,1:T(8,128)(2,1)S(1)} %get-tuple-element.22) | copy-start | bytes 2359300
  285.2 8.1 %copy-start.7 = (bf16[64,2,16,192]{3,2,0,1:T(8,128)(2,1)}, bf16[64,2,16,192]{3,2,0,1:T(8,128)(2,1)S(1)}, u32[]{:S(2)}) copy-start(bf16[64,2,16,192]{3,2,0,1:T(8,128)(2,1)S(1)} %get-tuple-element.23) | copy-start | bytes 2359300
  304.8 27.7 %copy-start.6 = (bf16[64,2,16,192]{3,2,0,1:T(8,128)(2,1)S(1)}, bf16[64,2,16,192]{3,2,0,1:T(8,128)(2,1)}, u32[]{:S(2)}) copy-start(bf16[64,2,16,192]{3,2,0,1:T(8,128)(2,1)} %copy-done.5) | copy-start | bytes 2359300
  317.8 74.6 %all-to-all-start.4 = ((bf16[64,1,32]{2,1,0:T(2,128)(2,1)}), bf16[64,1,32]{2,1,0:T(2,128)(2,1)S(1)}, u32[]{:S(2)}, u32[]{:S(2)}) async-start(bf16[64,1,32]{2,1,0:T(2,128)(2,1)} %copy.73), calls=%async_computation.5 | async-start | bytes 65536 | tf_op jit(solution)/shard_map/all_to_all | solution.py:81
  392.4 11.0 %copy-start.8 = (bf16[64,2,16,192]{3,2,0,1:T(8,128)(2,1)S(1)}, bf16[64,2,16,192]{3,2,0,1:T(8,128)(2,1)}, u32[]{:S(2)}) copy-start(bf16[64,2,16,192]{3,2,0,1:T(8,128)(2,1)} %copy-done.7) | copy-start | bytes 2359300
  392.4 62.1 %all-to-all-start.3 = ((bf16[64,32,512]{2,1,0:T(8,128)(2,1)}), bf16[64,32,512]{2,1,0:T(8,128)(2,1)}, u32[]{:S(2)}, u32[]{:S(2)}) async-start(bf16[64,32,512]{2,1,0:T(8,128)(2,1)} %bitcast.113), calls=%async_computation.4 | async-start | bytes 4194304 | tf_op jit(solution)/shard_map/all_to_all | solution.py:74
  403.4 6.5 %copy-start.11 = (bf16[64,2,16,192]{3,2,0,1:T(8,128)(2,1)S(1)}, bf16[64,2,16,192]{3,2,0,1:T(8,128)(2,1)}, u32[]{:S(2)}) copy-start(bf16[64,2,16,192]{3,2,0,1:T(8,128)(2,1)} %get-tuple-element.21) | copy-start | bytes 2359300
  458.6 10.4 %copy-start.1 = (bf16[2,192,2048]{2,1,0:T(8,128)(2,1)S(1)}, bf16[2,192,2048]{2,1,0:T(8,128)(2,1)}, u32[]{:S(2)}) copy-start(bf16[2,192,2048]{2,1,0:T(8,128)(2,1)} %param.11) | copy-start | bytes 4718596
Sparse Core Ops, SparseCore 0:
  105.2 82.0 all-gather.4
  189.1 86.6 all-gather.2
  305.0 84.1 reduce-scatter.1
where the time goes:
time: 476 us
  waiting for transfers between devices  156 us (33%)
  blocking collectives  148 us (31%)
  local copies, waits for them, and re-layouts  61.4 us (13%)
  matrix products  58.3 us (12%)
  starting transfers between devices  25.9 us (5%)
  between operations  14 us (3%)
  other arithmetic  11.9 us (2%)
    all_gather x1, waiting for transfers between devices, per_device(): lax.all_gather(sent_d, 'half', axis=2, tiled=True)  73.4 us
    all_to_all x1, blocking collectives, per_device(): lax.all_to_all(pack(tokens), 'expert', split_axis=0, concat_axis=0, tiled...  64.3 us
    all_to_all x1, blocking collectives, per_device(): lax.all_to_all(pack(cotangent), 'expert', split_axis=0, concat_axis=0, ti...  57.2 us
    reduce_scatter x1, waiting for transfers between devices, per_device(): lax.psum_scatter(part.astype(jnp.float32).astype(jnp.bfloat16), 'half', s...  50.2 us
    all_to_all x1, waiting for transfers between devices, per_device(): lax.all_to_all(summed.reshape(groups, local_exp * capacity, quarter).asty...  32.1 us
    gather x2, local copies, waits for them, and re-layouts, pack(): rows[token_of]  18.4 us
    all_to_all x1, blocking collectives, per_device(): lax.all_to_all(slot_prob, 'expert', split_axis=0, concat_axis=0, tiled=True)  14.9 us
    all_to_all x1, starting transfers between devices, per_device(): lax.all_to_all(total_score.reshape(groups, local_exp * capacity).astype(j...  14.8 us
  transfers between devices with their start and end apart: 5, of which 3 were waited for; matrix products, arithmetic and copies ran while one was open for 11% of the time, Pallas kernels for 0%

commit v1 on v0

--- a/solution.py
+++ b/solution.py
@@ -2,6 +2,22 @@
 import jax.numpy as jnp
 from jax import lax
 from jax.sharding import PartitionSpec as P
+
+
+def gather_around(x, axis, dim):
+    ways, here, lap = (lax.axis_size(axis), lax.axis_index(axis), x.shape[dim])
+    shape = [n * ways if d == dim else n for d, n in enumerate(x.shape)]
+    full = lax.dynamic_update_slice_in_dim(jnp.zeros(shape, x.dtype), x, here * lap, axis=dim)
+    going_up = going_down = x
+    for far in range(1, ways // 2 + 1):
+        going_up = lax.ppermute(going_up, axis, [(d, (d + 1) % ways) for d in range(ways)])
+        full = lax.dynamic_update_slice_in_dim(full, going_up, (here - far) % ways * lap, axis=dim)
+        if 2 * far < ways:
+            going_down = lax.ppermute(going_down, axis, [(d, (d - 1) % ways) for d in range(ways)])
+            full = lax.dynamic_update_slice_in_dim(
+                full, going_down, (here + far) % ways * lap, axis=dim
+            )
+    return full
 
 
 def per_device(tokens, cotangent, route, prob, w_gate, w_up, w_down):
@@ -35,7 +51,7 @@
     )
     recv_x, recv_d = (
         lax.all_gather(sent_x, "half", axis=2, tiled=True),
-        lax.all_gather(sent_d, "half", axis=2, tiled=True),
+        gather_around(sent_d, "half", 2),
     )
     width = recv_x.shape[2]
     xin = recv_x.reshape(groups, local_exp, capacity, width)

time: 476 us -> 502 us (1.055); the launches traced: 476 us -> 492 us
  local copies, waits for them, and re-layouts: 61.4 us -> 82.5 us
  waiting for transfers between devices: 156 us -> 141 us
  matrix products: 58.3 us -> 73 us
  blocking collectives: 148 us -> 136 us
  starting transfers between devices: 25.9 us -> 33.1 us
    all_gather x1 -> x0, waiting for transfers between devices: 73.4 us -> none  [per_device(): lax.all_gather(sent_d, 'half', axis=2, tiled=True)]
    ppermute x0 -> x3, waiting for transfers between devices: none -> 67.1 us  [the longest x2 67.1 us: gather_around(): lax.ppermute(going_up, axis, [(d, (d + 1) % ways) for d in range(ways)])]
    all_to_all x1, waiting for transfers between devices: 32.1 us -> 8.55 us  [per_device(): lax.all_to_all(summed.reshape(groups, local_exp * capacity, quarter).asty...]
    dynamic_update_slice x0 -> x4, local copies, waits for them, and re-layouts: none -> 16.7 us  [the longest x2 8.36 us: gather_around(): lax.dynamic_update_slice_in_dim(full, going_up, (here - far) % ways * lap...]
    all_to_all x1 -> x0, blocking collectives: 14.9 us -> none  [per_device(): lax.all_to_all(slot_prob, 'expert', split_axis=0, concat_axis=0, tiled=True)]
    all_to_all x0 -> x1, starting transfers between devices: none -> 10.7 us  [per_device(): lax.all_to_all(slot_prob, 'expert', split_axis=0, concat_axis=0, tiled=True)]
    all_to_all x0 -> x1, waiting for transfers between devices: none -> 8.93 us  [per_device(): lax.all_to_all(slot_prob, 'expert', split_axis=0, concat_axis=0, tiled=True)]
    dot_general x1, matrix products: 6.42 us -> 14.4 us  [per_device(): jnp.einsum('gecf,gecd->efd', dgate, xin, preferred_element_type=jnp.float32)]
  transfers between devices with their start and end apart: 5 -> 8, of which waited for: 3 -> 4; matrix products, arithmetic and copies ran while one was open for 11% -> 16% of each run, Pallas kernels for 0% -> 0%
where the time goes in v1:
time: 502 us; the launch traced here: 492 us
  waiting for transfers between devices  141 us (28%)
  blocking collectives  136 us (27%)
  local copies, waits for them, and re-layouts  82.5 us (16%)
  matrix products  73 us (15%)
  starting transfers between devices  33.1 us (7%)
  between operations  14.5 us (3%)
  other arithmetic  11.7 us (2%)
    ppermute x2, waiting for transfers between devices, gather_around(): lax.ppermute(going_up, axis, [(d, (d + 1) % ways) for d in range(ways)])  67.1 us
    all_to_all x1, blocking collectives, per_device(): lax.all_to_all(pack(tokens), 'expert', split_axis=0, concat_axis=0, tiled...  64.3 us
    all_to_all x1, blocking collectives, per_device(): lax.all_to_all(pack(cotangent), 'expert', split_axis=0, concat_axis=0, ti...  57.2 us
    reduce_scatter x1, waiting for transfers between devices, per_device(): lax.psum_scatter(part.astype(jnp.float32).astype(jnp.bfloat16), 'half', s...  56.5 us
    gather x2, local copies, waits for them, and re-layouts, pack(): rows[token_of]  18.3 us
    psum x1, blocking collectives, per_device(): total_score = lax.psum(score, 'half')  14.5 us
    dot_general x1, matrix products, per_device(): jnp.einsum('gecf,gecd->efd', dgate, xin, preferred_element_type=jnp.float32)  14.4 us
    dot_general x1, matrix products, per_device(): jnp.einsum('gecf,gecd->efd', dup, xin, preferred_element_type=jnp.float32)  14.1 us
  transfers between devices with their start and end apart: 8, of which 4 were waited for; matrix products, arithmetic and copies ran while one was open for 16% of the time, Pallas kernels for 0%

profile of v1, /device:TPU:1, one launch (start us, length us, event | category | flops | bytes accessed | tf_op | source)
XLA Modules:
  0.0 491.9 jit_solution(14415632511873597928)
XLA Ops:
  7.2 0.0 copy-start
  7.2 0.0 all-gather.2.cloned.1.call-start
  7.2 0.9 copy.74
  8.2 0.1 eq.33
  8.2 0.1 eq.29
  8.3 0.7 broadcast_multiply_fusion
  9.0 0.1 copy.76
  9.1 0.2 fusion.35
  9.4 0.1 copy.77
  9.5 0.1 copy.73
  9.6 0.1 mul.73
  9.7 0.4 fusion.34
  10.1 4.3 scatter_custom_fusion.1
  14.5 0.0 copy-start.3
  14.5 9.1 %gather_fusion.2 = bf16[2048,512]{1,0:T(8,128)(2,1)} fusion(bf16[128,512]{1,0:T(8,128)(2,1)S(1)} %copy-done.2, s32[2048]{0:T(1024)S(1)} %get-tuple-element.25), kind=kCustom, calls=%fused_computation.2 | custom fusion | bytes 4202496 | tf_op jit(solution)/shard_map/gather | solution.py:44
  23.6 9.2 %gather_fusion.1 = bf16[2048,512]{1,0:T(8,128)(2,1)} fusion(bf16[128,512]{1,0:T(8,128)(2,1)S(1)} %copy-done.3, s32[2048]{0:T(1024)S(1)} %get-tuple-element.25), kind=kCustom, calls=%fused_computation.1 | custom fusion | bytes 4202496 | tf_op jit(solution)/shard_map/gather | solution.py:44
  32.8 4.3 scatter_custom_fusion
  37.2 0.1 broadcast_in_dim.52
  37.3 3.4 broadcast_select_fusion
  40.6 64.3 %all_to_all.31 = bf16[64,32,512]{2,1,0:T(8,128)(2,1)} all-to-all(bf16[64,32,512]{2,1,0:T(8,128)(2,1)S(1)} %get-tuple-element.26), channel_id=1, replica_groups=mesh['expert'=64,'half'=4] {'expert'}, dimensions={0} | all-to-all | bytes 4194304 | tf_op jit(solution)/shard_map/all_to_all | solution.py:48
  104.9 0.0 all-gather.2.cloned.1.call-update
  105.0 0.0 copy-start.7
  105.0 57.2 %all_to_all.32 = bf16[64,32,512]{2,1,0:T(8,128)(2,1)} all-to-all(bf16[64,32,512]{2,1,0:T(8,128)(2,1)} %get-tuple-element.27), channel_id=1, replica_groups=mesh['expert'=64,'half'=4] {'expert'}, dimensions={0} | all-to-all | bytes 4194304 | tf_op jit(solution)/shard_map/all_to_all | solution.py:49
  162.1 1.2 collective-permute-start
  163.4 1.5 collective-permute-start.1
  164.8 67.1 %collective-permute-done = bf16[64,32,512]{2,1,0:T(8,128)(2,1)} collective-permute-done((bf16[64,32,512]{2,1,0:T(8,128)(2,1)}, bf16[64,32,512]{2,1,0:T(8,128)(2,1)}, u32[]{:S(2)}, u32[]{:S(2)}) %collective-permute-start) | collective-permute-done | bytes 2097184 | tf_op jit(solution)/shard_map/ppermute | solution.py:13
  231.9 0.1 copy.78
  232.0 0.1 reshape.125
  232.1 13.1 %gather_fusion = bf16[2048]{0:T(1024)(128)(2,1)S(1)} fusion(bf16[1024]{0:T(1024)(128)(2,1)S(1)} %reshape.125, s32[2048]{0:T(1024)S(1)} %get-tuple-element.24), kind=kCustom, calls=%fused_computation | custom fusion | bytes 16384 | tf_op jit(solution)/shard_map/gather | solution.py:40
  245.2 0.7 all_to_all.25
  245.9 10.7 %all-to-all-start = ((bf16[64,1,32]{2,1,0:T(2,128)(2,1)}), bf16[64,1,32]{2,1,0:T(2,128)(2,1)S(1)}, u32[]{:S(2)}, u32[]{:S(2)}) async-start(bf16[64,1,32]{2,1,0:T(2,128)(2,1)} %all_to_all.25), calls=%async_computation | async-start | bytes 65536 | tf_op jit(solution)/shard_map/all_to_all | solution.py:50
  256.6 0.2 reduce-scatter.2.cloned.1.call-start
  256.9 8.9 %all-to-all-done = bf16[64,1,32]{2,1,0:T(2,128)(2,1)S(1)} async-done(((bf16[64,1,32]{2,1,0:T(2,128)(2,1)}), bf16[64,1,32]{2,1,0:T(2,128)(2,1)S(1)}, u32[]{:S(2)}, u32[]{:S(2)}) %all-to-all-start) | async-done | bytes 4128 | tf_op jit(solution)/shard_map/all_to_all | solution.py:50
  265.8 0.1 copy.80
  265.9 4.3 broadcast_in_dim.51
  270.2 4.2 copy_dynamic-update-slice_fusion.3
  274.4 4.2 copy_dynamic-update-slice_fusion.2
  278.5 4.2 copy_dynamic-update-slice_fusion.1
  282.7 4.2 copy_dynamic-update-slice_fusion
  286.9 5.9 %fusion.7 = f32[2,64,16,192]{3,2,1,0:T(8,128)S(1)} fusion(bf16[64,2,16,2048]{3,2,1,0:T(8,128)(2,1)} %bitcast.114, bf16[2,192,2048]{2,1,0:T(8,128)(2,1)S(1)} %copy-done), kind=kOutput, calls=%fused_computation.16 | convolution fusion | flops 1610612736 | bytes 11534336 | tf_op jit(solution)/shard_map/gecd,efd->gecf/dot_general | solution.py:60
  292.8 0.4 copy-done.8
  293.2 2.3 fusion.9
  295.5 9.6 %fusion.23 = (f32[64,2,16]{0,2,1:T(8,128)S(1)}, bf16[64,2,16,192]{3,0,2,1:T(8,128)(2,1)}, bf16[64,2,16,192]{3,0,2,1:T(8,128)(2,1)S(1)}, bf16[64,2,16,192]{3,0,2,1:T(8,128)(2,1)S(1)}) fusion(f32[2,64,16,192]{3,2,1,0:T(8,128)S(1)} %fusion.9, f32[2,64,16,192]{3,2,1,0:T(8,128)S(1)} %fusion.7, f32[64,2,16]{0,2,1:T(8,128)S(1)} %convert.3, ...), kind=kOutput, calls=%fused_computation.40 | convolution fusion | flops 1618081792 | bytes 15482880 | tf_op jit(solution)/shard_map/gecd,efd->gecf/dot_general | solution.py:65
  305.2 8.3 %fusion.24 = f32[2,64,16,2048]{3,2,1,0:T(8,128)} fusion(bf16[2,192,2048]{2,1,0:T(8,128)(2,1)S(1)} %copy-done, bf16[64,2,16,192]{3,0,2,1:T(8,128)(2,1)S(1)} %get-tuple-element.22), kind=kOutput, calls=%fused_computation.48 | convolution fusion | flops 1610612736 | bytes 19136512 | tf_op jit(solution)/shard_map/gecf,efd->gecd/dot_general | solution.py:80
  313.4 11.8 %fusion = bf16[64,2,16,2048]{3,2,0,1:T(8,128)(2,1)} fusion(f32[2,64,16,2048]{3,2,1,0:T(8,128)} %fusion.24, bf16[2,192,2048]{2,1,0:T(8,128)(2,1)S(1)} %copy-done.4, bf16[64,2,16,192]{3,0,2,1:T(8,128)(2,1)S(1)} %get-tuple-element.23), kind=kOutput, calls=%fused_computation.9 | convolution fusion | flops 1619001344 | bytes 27525120 | tf_op jit(solution)/shard_map/gecf,efd->gecd/dot_general | solution.py:82
  325.2 0.0 reduce-scatter.2.cloned.1.call-update
  325.2 14.5 %psum.7 = bf16[64,2,16]{0,2,1:T(8,128)(2,1)S(1)} all-reduce(f32[64,2,16]{0,2,1:T(8,128)S(1)} %get-tuple-element.20), channel_id=1, replica_groups=mesh['expert'=64,'half'=4] {'half'}, use_global_device_ids=true, to_apply=%region_8.9 | all-reduce | flops 2048 | bytes 12288 | tf_op jit(solution)/shard_map/psum | solution.py:87
  339.7 0.7 copy.94
  340.4 8.2 %all-to-all-start.4 = ((bf16[64,1,32]{2,1,0:T(2,128)(2,1)}), bf16[64,1,32]{2,1,0:T(2,128)(2,1)S(1)}, u32[]{:S(2)}, u32[]{:S(2)}) async-start(bf16[64,1,32]{2,1,0:T(2,128)(2,1)} %copy.94), calls=%async_computation.5 | async-start | bytes 65536 | tf_op jit(solution)/shard_map/all_to_all | solution.py:97
  348.7 56.5 %reduce-scatter.2.cloned.1.call-done = bf16[64,2,16,512]{3,2,0,1:T(8,128)(2,1)} async-done(((bf16[64,2,16,2048]{3,2,0,1:T(8,128)(2,1)}), bf16[64,2,16,512]{3,2,0,1:T(8,128)(2,1)}) %reduce-scatter.2.cloned.1.call-update) | async-done | bytes 2097168 | tf_op jit(solution)/shard_map/reduce_scatter | solution.py:84
  405.2 3.1 copy.91
  408.4 11.3 %all-to-all-start.3 = ((bf16[64,32,512]{2,1,0:T(8,128)(2,1)}), bf16[64,32,512]{2,1,0:T(8,128)(2,1)}, u32[]{:S(2)}, u32[]{:S(2)}) async-start(bf16[64,32,512]{2,1,0:T(8,128)(2,1)} %bitcast.107), calls=%async_computation.4 | async-start | bytes 4194304 | tf_op jit(solution)/shard_map/all_to_all | solution.py:90
  419.7 14.1 %bitcast_convert_fusion.1 = bf16[2,192,2048]{2,1,0:T(8,128)(2,1)} fusion(bf16[64,2,16,192]{3,0,2,1:T(8,128)(2,1)S(1)} %copy-done.6, bf16[64,2,16,2048]{3,2,1,0:T(8,128)(2,1)} %bitcast.115), kind=kOutput, calls=%fused_computation.21 | convolution fusion | flops 1611399168 | bytes 10747904 | tf_op jit(solution)/shard_map/gecf,gecd->efd/dot_general | solution.py:77
  433.8 14.4 %bitcast_convert_fusion.2 = bf16[2,192,2048]{2,1,0:T(8,128)(2,1)} fusion(bf16[64,2,16,192]{3,0,2,1:T(8,128)(2,1)S(1)} %get-tuple-element.22, bf16[64,2,16,2048]{3,2,1,0:T(8,128)(2,1)} %bitcast.116), kind=kOutput, calls=%fused_computation.22 | convolution fusion | flops 1611399168 | bytes 10747904 | tf_op jit(solution)/shard_map/gecf,gecd->efd/dot_general | solution.py:74
  448.2 6.6 %bitcast_convert_fusion = bf16[2,192,2048]{2,1,0:T(8,128)(2,1)} fusion(bf16[64,2,16,192]{3,0,2,1:T(8,128)(2,1)S(1)} %copy-done.10, bf16[64,2,16,2048]{3,0,2,1:T(8,128)(2,1)} %bitcast.7, f32[64,2,16]{0,2,1:T(8,128)S(1)} %convert.3), kind=kOutput, calls=%fused_computation.20 | convolution fusion | flops 1623982080 | bytes 10756096 | tf_op jit(solution)/shard_map/gecf,gecd->efd/dot_general | solution.py:71
  454.8 0.1 convert_reduce_fusion
  454.9 0.1 reshape.135
  454.9 6.1 %gather_fusion.4 = f32[1024]{0:T(1024)S(1)} fusion(f32[2048]{0:T(1024)S(1)} %reshape.135, s32[1024]{0:T(1024)S(1)} %broadcast_clamp_fusion), kind=kCustom, calls=%fused_computation.4 | custom fusion | bytes 12288 | tf_op jit(solution)/shard_map/gather | solution.py:107
  461.1 0.1 reshape.131
  461.2 0.7 copy.97
  461.9 8.5 %all-to-all-done.3 = bf16[64,32,512]{2,1,0:T(8,128)(2,1)} async-done(((bf16[64,32,512]{2,1,0:T(8,128)(2,1)}), bf16[64,32,512]{2,1,0:T(8,128)(2,1)}, u32[]{:S(2)}, u32[]{:S(2)}) %all-to-all-start.3) | async-done | bytes 2097184 | tf_op jit(solution)/shard_map/all_to_all | solution.py:90
  470.4 4.1 bitcast_convert_fusion.3
  474.5 7.6 %gather_fusion.3 = f32[1024,512]{1,0:T(8,128)} fusion(f32[2048,512]{1,0:T(8,128)} %bitcast_convert_fusion.3, s32[1024]{0:T(1024)S(1)} %broadcast_clamp_fusion), kind=kCustom, calls=%fused_computation.3 | custom fusion | bytes 4198400 | tf_op jit(solution)/shard_map/gather | solution.py:105
  482.1 2.8 bitcast_reduce_fusion
  (34 shorter events, 0.2 us)
Async XLA Ops:
  7.2 279.7 %copy-start = (bf16[2,192,2048]{2,1,0:T(8,128)(2,1)S(1)}, bf16[2,192,2048]{2,1,0:T(8,128)(2,1)}, u32[]{:S(2)}) copy-start(bf16[2,192,2048]{2,1,0:T(8,128)(2,1)} %param.11) | copy-start | bytes 4718596
  7.2 7.3 %copy-start.2 = (bf16[128,512]{1,0:T(8,128)(2,1)S(1)}, bf16[128,512]{1,0:T(8,128)(2,1)}, u32[]{:S(2)}) copy-start(bf16[128,512]{1,0:T(8,128)(2,1)} %param.7) | copy-start | bytes 393220
  7.2 279.7 %all-gather.2.cloned.1.call-start = ((), (), s32[]{:S(2)}) async-start(), calls=%async_computation.6 | async-start | bytes 10485760 | tf_op jit(solution)/shard_map/all_gather | solution.py:53
  14.5 9.2 %copy-start.3 = (bf16[128,512]{1,0:T(8,128)(2,1)S(1)}, bf16[128,512]{1,0:T(8,128)(2,1)}, u32[]{:S(2)}) copy-start(bf16[128,512]{1,0:T(8,128)(2,1)} %param.8) | copy-start | bytes 393220
  105.0 126.9 %copy-start.7 = (bf16[128,8]{0,1:T(8,128)(2,1)S(1)}, bf16[128,8]{0,1:T(8,128)(2,1)}, u32[]{:S(2)}) copy-start(bf16[128,8]{0,1:T(8,128)(2,1)} %param.10) | copy-start | bytes 6148
  162.1 69.7 %collective-permute-start = (bf16[64,32,512]{2,1,0:T(8,128)(2,1)}, bf16[64,32,512]{2,1,0:T(8,128)(2,1)}, u32[]{:S(2)}, u32[]{:S(2)}) collective-permute-start(bf16[64,32,512]{2,1,0:T(8,128)(2,1)} %all_to_all.32), channel_id=1, source_target_pairs={{0,1},{1,2},{2,3},{3,0},{4,5},{5,6},{6,7},{7,4},{8,9},{9,10},{10,1... | collective-permute-start | bytes 6291464 | tf_op jit(solution)/shard_map/ppermute | solution.py:13
  163.4 115.2 %collective-permute-start.1 = (bf16[64,32,512]{2,1,0:T(8,128)(2,1)}, bf16[64,32,512]{2,1,0:T(8,128)(2,1)}, u32[]{:S(2)}, u32[]{:S(2)}) collective-permute-start(bf16[64,32,512]{2,1,0:T(8,128)(2,1)} %all_to_all.32), channel_id=1, source_target_pairs={{0,3},{1,0},{2,1},{3,2},{4,7},{5,4},{6,5},{7,6},{8,11},{9,8},{10,9... | collective-permute-start | bytes 6291464 | tf_op jit(solution)/shard_map/ppermute | solution.py:16
  231.9 50.8 %collective-permute-start.2 = (bf16[64,32,512]{2,1,0:T(8,128)(2,1)}, bf16[64,32,512]{2,1,0:T(8,128)(2,1)}, u32[]{:S(2)}, u32[]{:S(2)}) collective-permute-start(bf16[64,32,512]{2,1,0:T(8,128)(2,1)} %collective-permute-done), channel_id=1, source_target_pairs={{0,1},{1,2},{2,3},{3,0},{4,5},{5,6},{6,7},{7,4},{8,9},{9,10},{10,1... | collective-permute-start | bytes 6291464 | tf_op jit(solution)/shard_map/ppermute | solution.py:13
  245.9 19.9 %all-to-all-start = ((bf16[64,1,32]{2,1,0:T(2,128)(2,1)}), bf16[64,1,32]{2,1,0:T(2,128)(2,1)S(1)}, u32[]{:S(2)}, u32[]{:S(2)}) async-start(bf16[64,1,32]{2,1,0:T(2,128)(2,1)} %all_to_all.25), calls=%async_computation | async-start | bytes 65536 | tf_op jit(solution)/shard_map/all_to_all | solution.py:50
  256.6 148.6 %reduce-scatter.2.cloned.1.call-start = ((), (), s32[]{:S(2)}) async-start(), calls=%async_computation.7 | async-start | bytes 10485760 | tf_op jit(solution)/shard_map/reduce_scatter | solution.py:84
  286.9 5.9 %copy-start.4 = (bf16[2,192,2048]{2,1,0:T(8,128)(2,1)S(1)}, bf16[2,192,2048]{2,1,0:T(8,128)(2,1)}, u32[]{:S(2)}) copy-start(bf16[2,192,2048]{2,1,0:T(8,128)(2,1)} %param.12) | copy-start | bytes 4718596
  286.9 6.3 %copy-start.8 = (bf16[64,32,2048]{2,1,0:T(8,128)(2,1)S(1)}, bf16[64,32,2048]{2,1,0:T(8,128)(2,1)}, u32[]{:S(2)}) copy-start(bf16[64,32,2048]{2,1,0:T(8,128)(2,1)} %all-gather.2.cloned.1.call-done) | copy-start | bytes 25165828
  293.2 2.4 copy-start.9
  305.2 8.3 %copy-start.5 = (bf16[64,2,16,192]{3,0,2,1:T(8,128)(2,1)}, bf16[64,2,16,192]{3,0,2,1:T(8,128)(2,1)S(1)}, u32[]{:S(2)}) copy-start(bf16[64,2,16,192]{3,0,2,1:T(8,128)(2,1)S(1)} %get-tuple-element.23) | copy-start | bytes 2359300
  340.4 67.9 %all-to-all-start.4 = ((bf16[64,1,32]{2,1,0:T(2,128)(2,1)}), bf16[64,1,32]{2,1,0:T(2,128)(2,1)S(1)}, u32[]{:S(2)}, u32[]{:S(2)}) async-start(bf16[64,1,32]{2,1,0:T(2,128)(2,1)} %copy.94), calls=%async_computation.5 | async-start | bytes 65536 | tf_op jit(solution)/shard_map/all_to_all | solution.py:97
  408.4 11.3 %copy-start.6 = (bf16[64,2,16,192]{3,0,2,1:T(8,128)(2,1)S(1)}, bf16[64,2,16,192]{3,0,2,1:T(8,128)(2,1)}, u32[]{:S(2)}) copy-start(bf16[64,2,16,192]{3,0,2,1:T(8,128)(2,1)} %copy-done.5) | copy-start | bytes 2359300
  408.4 62.0 %all-to-all-start.3 = ((bf16[64,32,512]{2,1,0:T(8,128)(2,1)}), bf16[64,32,512]{2,1,0:T(8,128)(2,1)}, u32[]{:S(2)}, u32[]{:S(2)}) async-start(bf16[64,32,512]{2,1,0:T(8,128)(2,1)} %bitcast.107), calls=%async_computation.4 | async-start | bytes 4194304 | tf_op jit(solution)/shard_map/all_to_all | solution.py:90
  433.8 14.4 %copy-start.10 = (bf16[64,2,16,192]{3,0,2,1:T(8,128)(2,1)S(1)}, bf16[64,2,16,192]{3,0,2,1:T(8,128)(2,1)}, u32[]{:S(2)}) copy-start(bf16[64,2,16,192]{3,0,2,1:T(8,128)(2,1)} %get-tuple-element.21) | copy-start | bytes 2359300
  474.5 10.4 %copy-start.1 = (bf16[2,192,2048]{2,1,0:T(8,128)(2,1)S(1)}, bf16[2,192,2048]{2,1,0:T(8,128)(2,1)}, u32[]{:S(2)}) copy-start(bf16[2,192,2048]{2,1,0:T(8,128)(2,1)} %param.11) | copy-start | bytes 4718596
Sparse Core Ops, SparseCore 0:
  105.1 102.4 all-gather.1
  325.3 79.8 reduce-scatter.1
